TPU v7x, 256 devices: a whole 4x4x8 slice. The times are simulated.
256 devices in a mesh: group: 16 (over x_lo, z), shard: 16 (over x_hi, y, core).
Axes of the slice: x: 4 (x_hi: 2, x_lo: 2; x = x_hi * 2 + x_lo), y: 4, z: 8, core: 2. Of those that a mesh axis runs over, the one named last changes fastest.
Arguments:
- queries: bfloat16 [2, 3, 32768, 512], P(None, None, ('group', 'shard')), may hold values from -6 to 6
- key_tokens: bfloat16 [2, 3, 32768, 512], P(None, None, ('group', 'shard')), may hold values from -24 to 24
- value_tokens: bfloat16 [2, 3, 32768, 512], P(None, None, ('group', 'shard')), may hold values from -24 to 24
- token_rate: float32 [2, 3, 32768], P(None, None, ('group', 'shard')), may hold values from 0.1 to 1
- state_in: float32 [16, 3, 512, 3, 512], P('group', None, 'shard'), may hold values from -0.25 to 0.25
- init_state: float32 [3, 512, 3, 512], P(None, 'shard'), may hold values from -0.25 to 0.25
- norm_gain: float32 [3, 512], replicated, may hold values from 0.25 to 2.5
Outputs:
- head_output: bfloat16 [2, 3, 32768, 512], P(None, None, ('group', 'shard'))
- state_out: float32 [16, 3, 512, 3, 512], P('group', None, 'shard')
All inputs are finite; a program needn't handle non-finite values.
Results may differ from a plain program's by a relative error of at most 0.011.
Values may be sent and summed in bfloat16 or wider, within the bound.
A program may use at most 128 MiB of HBM per device.

v0:
```python
import jax
import jax.numpy as jnp
from jax import lax
from jax.sharding import PartitionSpec as P

epsilon = 1e-06


def shifted(value, axis, steps):
    count = lax.axis_size(axis)
    leading, last = (max(0, -steps), min(count, count - steps))
    return lax.ppermute(value, axis, [(source, source + steps) for source in range(leading, last)])


def forward(rows, packed):
    pre_gate = jnp.dot(rows, packed[:, 0], preferred_element_type=jnp.float32)
    pre_up = jnp.dot(rows, packed[:, 1], preferred_element_type=jnp.float32)
    sigmoid_gate = jax.nn.sigmoid(pre_gate)
    hidden = (pre_gate * sigmoid_gate * pre_up).astype(jnp.bfloat16)
    produced = lax.dot_general(
        hidden, packed[:, 2], (((1,), (1,)), ((), ())), preferred_element_type=jnp.float32
    )
    return (pre_gate, pre_up, sigmoid_gate, hidden, produced)


def on_device(queries, key_tokens, value_tokens, token_rate, state_in, init_state, norm_gain):
    head_count = queries.shape[1]
    token_rows = queries.shape[2]
    span = token_rows * lax.axis_size("shard")

    def head_pass(slot_index, head_index, packed, shard_weights):
        query_rows = queries[slot_index, head_index]
        key_rows = key_tokens[slot_index, head_index]
        value_rows = value_tokens[slot_index, head_index]
        rate_row = token_rate[slot_index, head_index]
        applied = forward(query_rows, packed)[4]
        normed = (
            applied
            * lax.rsqrt(jnp.mean(applied * applied, axis=-1, keepdims=True) + epsilon)
            * norm_gain[head_index]
        )
        pre_gate, pre_up, sigmoid_gate, hidden, guess = forward(key_rows, packed)
        error = (rate_row[:, None] * (guess - value_rows.astype(jnp.float32))).astype(jnp.bfloat16)
        back_hidden = jnp.dot(error, packed[:, 2], preferred_element_type=jnp.float32)
        grad_gate = (
            back_hidden * pre_up * sigmoid_gate * (1.0 + pre_gate * (1.0 - sigmoid_gate))
        ).astype(jnp.bfloat16)
        grad_up = (back_hidden * pre_gate * sigmoid_gate).astype(jnp.bfloat16)
        contract = (((0,), (0,)), ((), ()))
        gate_part = lax.dot_general(
            key_rows, grad_gate, contract, preferred_element_type=jnp.float32
        )
        up_part = lax.dot_general(key_rows, grad_up, contract, preferred_element_type=jnp.float32)
        down_part = lax.dot_general(error, hidden, contract, preferred_element_type=jnp.float32)
        summed = lax.psum_scatter(
            jnp.stack([gate_part, up_part, down_part], axis=1),
            "shard",
            scatter_dimension=0,
            tiled=True,
        )
        updated = shard_weights - summed / float(span)
        return (normed.astype(jnp.bfloat16), updated)

    def slot_pass(slot_index, shards):
        outputs = []
        updates = []
        arrivals = []
        for head_index in range(head_count):
            packed = lax.all_gather(
                shards[head_index].astype(jnp.bfloat16), "shard", axis=0, tiled=True
            )
            normed, updated = head_pass(slot_index, head_index, packed, shards[head_index])
            outputs.append(normed)
            updates.append(updated)
        return (outputs, updates, arrivals)

    first_outputs, middle, arrivals = slot_pass(0, state_in[0])
    arrived = shifted(jnp.stack(middle, axis=0).astype(jnp.bfloat16), "group", 1).astype(
        jnp.float32
    )
    arrived = jnp.where(lax.axis_index("group") == 0, init_state, arrived)
    second_outputs, final, unused = slot_pass(1, arrived)
    head_output = jnp.stack(
        [jnp.stack(first_outputs, axis=0), jnp.stack(second_outputs, axis=0)], axis=0
    )
    state_out = jnp.stack(final, axis=0)[None]
    return (head_output, state_out)


def solution(mesh):
    in_specs = (
        P(None, None, ("group", "shard"), None),
        P(None, None, ("group", "shard"), None),
        P(None, None, ("group", "shard"), None),
        P(None, None, ("group", "shard")),
        P("group", None, "shard", None, None),
        P(None, "shard", None, None),
        P(),
    )
    out_specs = (P(None, None, ("group", "shard"), None), P("group", None, "shard", None, None))
    return jax.shard_map(
        on_device, mesh=mesh, in_specs=in_specs, out_specs=out_specs, check_vma=False
    )
```

profile of v0, /device:TPU:32, one launch (start us, length us, event | category | flops | bytes accessed | tf_op | source)
XLA Modules:
  0.0 756.1 jit_solution(18101220173649434521)
XLA Ops:
  7.2 1.9 bitcast_convert_fusion.2
  11.4 53.0 %all-gather.9.cloned.1.call-done = bf16[512,3,512]{2,0,1:T(8,128)(2,1)} async-done(((bf16[32,3,512]{2,0,1:T(8,128)(2,1)}), bf16[512,3,512]{2,0,1:T(8,128)(2,1)}) %all-gather.9.cloned.1.call-update) | async-done | bytes 1572880 | tf_op jit(solution)/shard_map/all_gather | solution.py:69
  64.5 1.4 fusion.30
  69.7 48.0 %all-gather.11.cloned.1.call-done = bf16[512,3,512]{2,0,1:T(8,128)(2,1)} async-done(((bf16[32,3,512]{2,0,1:T(8,128)(2,1)}), bf16[512,3,512]{2,0,1:T(8,128)(2,1)}) %all-gather.11.cloned.1.call-update) | async-done | bytes 1572880 | tf_op jit(solution)/shard_map/all_gather | solution.py:69
  117.8 1.4 fusion.33
  128.8 42.3 %all-gather.7.cloned.1.call-done = bf16[512,3,512]{2,0,1:T(8,128)(2,1)} async-done(((bf16[32,3,512]{2,0,1:T(8,128)(2,1)}), bf16[512,3,512]{2,0,1:T(8,128)(2,1)}) %all-gather.7.cloned.1.call-update) | async-done | bytes 1572880 | tf_op jit(solution)/shard_map/all_gather | solution.py:69
  171.1 1.4 fusion.27
  176.6 3.5 copy.30
  180.1 2.2 pad_maximum_fusion.2
  182.3 3.6 copy.36
  185.8 2.2 pad_maximum_fusion.1
  188.0 3.6 copy.33
  193.5 179.7 %all-reduce.13.cloned.1.call-done = (f32[512,3,512]{2,1,0:T(4,128)}, f32[512,3,512]{2,1,0:T(4,128)}, f32[512,3,512]{2,1,0:T(4,128)}) async-done(((f32[512,3,512]{2,1,0:T(4,128)}, f32[512,3,512]{2,1,0:T(4,128)}, f32[512,3,512]{2,1,0:T(4,128)}), (f32[512,3,512]{2,1,0:T(4,128)}, f32[512,3,512]{2,1,0:T(4,128)}, f32[512,3,512]{2,1,0:T(4,128)})) %all-reduce.13.cloned.1.call-update) | async-done | bytes 9437200
  375.7 3.6 collective-permute-start
  379.3 5.1 collective-permute-done
  387.6 49.3 %all-gather.15.cloned.1.call-done = bf16[512,3,512]{2,0,1:T(8,128)(2,1)} async-done(((bf16[32,3,512]{2,0,1:T(8,128)(2,1)}), bf16[512,3,512]{2,0,1:T(8,128)(2,1)}) %all-gather.15.cloned.1.call-update) | async-done | bytes 1572880 | tf_op jit(solution)/shard_map/all_gather | solution.py:69
  437.0 1.4 convolution_bitcast_fusion.21
  442.2 47.4 %all-gather.17.cloned.1.call-done = bf16[512,3,512]{2,0,1:T(8,128)(2,1)} async-done(((bf16[32,3,512]{2,0,1:T(8,128)(2,1)}), bf16[512,3,512]{2,0,1:T(8,128)(2,1)}) %all-gather.17.cloned.1.call-update) | async-done | bytes 1572880 | tf_op jit(solution)/shard_map/all_gather | solution.py:69
  500.6 42.3 %all-gather.13.cloned.1.call-done = bf16[512,3,512]{2,0,1:T(8,128)(2,1)} async-done(((bf16[32,3,512]{2,0,1:T(8,128)(2,1)}), bf16[512,3,512]{2,0,1:T(8,128)(2,1)}) %all-gather.13.cloned.1.call-update) | async-done | bytes 1572880 | tf_op jit(solution)/shard_map/all_gather | solution.py:69
  542.9 1.4 convolution_bitcast_fusion.23
  548.4 3.5 copy.44
  551.9 2.2 pad_maximum_fusion.5
  554.0 3.6 copy.54
  557.6 2.2 pad_maximum_fusion.4
  559.8 3.6 copy.49
  565.9 2.2 multiply_reduce_fusion.4
  569.2 2.2 multiply_reduce_fusion.3
  572.6 2.2 multiply_reduce_fusion.5
  575.9 2.2 multiply_reduce_fusion.1
  579.3 2.2 multiply_reduce_fusion
  582.7 1.5 multiply_reduce_fusion.2
  585.7 159.4 %all-reduce.11.cloned.1.call-done = (f32[512,3,512]{2,1,0:T(4,128)}, f32[512,3,512]{2,1,0:T(4,128)}, f32[512,3,512]{2,1,0:T(4,128)}) async-done(((f32[512,3,512]{2,1,0:T(4,128)}, f32[512,3,512]{2,1,0:T(4,128)}, f32[512,3,512]{2,1,0:T(4,128)}), (f32[512,3,512]{2,1,0:T(4,128)}, f32[512,3,512]{2,1,0:T(4,128)}, f32[512,3,512]{2,1,0:T(4,128)})) %all-reduce.11.cloned.1.call-update) | async-done | bytes 9437200
  (137 shorter events, 59.3 us)
Async XLA Ops:
  7.2 58.8 %copy-start = (bf16[2,3,128,512]{3,2,1,0:T(8,128)(2,1)S(1)}, bf16[2,3,128,512]{3,2,1,0:T(8,128)(2,1)}, u32[]{:S(2)}) copy-start(bf16[2,3,128,512]{3,2,1,0:T(8,128)(2,1)} %param.8) | copy-start | bytes 2359300
  7.2 57.3 %all-gather.9.cloned.1.call-start = ((), (), s32[]{:S(2)}) async-start(), calls=%async_computation.1 | async-start | bytes 1671168 | tf_op jit(solution)/shard_map/all_gather | solution.py:69
  9.1 108.6 %all-gather.11.cloned.1.call-start = ((), (), s32[]{:S(2)}) async-start(), calls=%async_computation.2 | async-start | bytes 1671168 | tf_op jit(solution)/shard_map/all_gather | solution.py:69
  9.9 161.2 %all-gather.7.cloned.1.call-start = ((), (), s32[]{:S(2)}) async-start(), calls=%async_computation | async-start | bytes 1671168 | tf_op jit(solution)/shard_map/all_gather | solution.py:69
  10.6 362.5 %all-reduce.13.cloned.1.call-start = ((), (), s32[]{:S(2)}) async-start(), calls=%async_computation.7 | async-start | bytes 25165824
  64.5 2.7 copy-start.4
  117.8 2.7 copy-start.6
  171.1 2.7 copy-start.8
  191.6 183.8 %copy-start.16 = (f32[1,3,32,3,512]{4,2,3,1,0:T(8,128)S(1)}, f32[1,3,32,3,512]{4,2,3,1,0:T(8,128)}, u32[]{:S(2)}) copy-start(f32[1,3,32,3,512]{4,2,3,1,0:T(8,128)} %param.11) | copy-start | bytes 1769476
  191.6 245.4 %all-gather.15.cloned.1.call-start = ((), (), s32[]{:S(2)}) async-start(), calls=%async_computation.4 | async-start | bytes 1671168 | tf_op jit(solution)/shard_map/all_gather | solution.py:69
  374.1 10.3 %copy-start.17 = (f32[3,32,3,512]{3,1,2,0:T(8,128)S(1)}, f32[3,32,3,512]{3,1,2,0:T(8,128)}, u32[]{:S(2)}) copy-start(f32[3,32,3,512]{3,1,2,0:T(8,128)} %param.12) | copy-start | bytes 1769476
  375.6 61.4 %copy-start.1 = (bf16[2,3,128,512]{3,2,1,0:T(8,128)(2,1)S(1)}, bf16[2,3,128,512]{3,2,1,0:T(8,128)(2,1)}, u32[]{:S(2)}) copy-start(bf16[2,3,128,512]{3,2,1,0:T(8,128)(2,1)} %param.8) | copy-start | bytes 2359300
  375.7 8.7 %collective-permute-start = (bf16[3,32,3,512]{3,1,2,0:T(8,128)(2,1)S(1)}, bf16[3,32,3,512]{3,1,2,0:T(8,128)(2,1)S(1)}, u32[]{:S(2)}, u32[]{:S(2)}) collective-permute-start(bf16[3,32,3,512]{3,1,2,0:T(8,128)(2,1)S(1)} %pad_maximum_fusion.7), channel_id=1, source_target_pairs={{0,16},{16,32},{32,48},{48,64},{64,80},{80,96},{96,112},{112,128},... | collective-permute-start | bytes 884744 | tf_op jit(solution)/shard_map/ppermute | solution.py:12
  384.5 0.8 copy-start.2
  386.1 103.5 %all-gather.17.cloned.1.call-start = ((), (), s32[]{:S(2)}) async-start(), calls=%async_computation.5 | async-start | bytes 1671168 | tf_op jit(solution)/shard_map/all_gather | solution.py:69
  386.7 156.2 %all-gather.13.cloned.1.call-start = ((), (), s32[]{:S(2)}) async-start(), calls=%async_computation.3 | async-start | bytes 1671168 | tf_op jit(solution)/shard_map/all_gather | solution.py:69
  387.4 357.7 %all-reduce.11.cloned.1.call-start = ((), (), s32[]{:S(2)}) async-start(), calls=%async_computation.6 | async-start | bytes 25165824
  437.0 2.7 copy-start.10
  489.6 2.7 copy-start.12
  542.9 2.7 copy-start.14
  563.3 1.4 copy-start.5
  565.9 2.2 copy-start.7
  569.2 2.2 copy-start.9
  572.6 2.2 copy-start.11
  575.9 2.2 copy-start.13
  579.3 2.2 copy-start.15
  582.6 1.6 copy-start.20
  582.6 1.6 copy-start.22
  582.6 1.7 copy-start.19
  582.7 1.7 copy-start.21
  582.7 1.8 copy-start.18
  584.7 163.4 %copy-start.3 = (f32[3,32,3,512]{3,1,2,0:T(8,128)S(1)}, f32[3,32,3,512]{3,1,2,0:T(8,128)}, u32[]{:S(2)}) copy-start(f32[3,32,3,512]{3,1,2,0:T(8,128)} %copy-done.2) | copy-start | bytes 1769476
  (2 other events, 1.4 us)
Sparse Core Ops, SparseCore 0:
  10.8 53.6 all-gather.8
  67.8 49.8 all-gather.10
  121.2 49.8 all-gather.6
  191.7 181.3 all-reduce.12
  386.2 50.7 all-gather.14
  439.6 49.8 all-gather.16
  492.9 49.8 all-gather.12
  563.5 181.5 all-reduce.10
where the time goes:
time: 757 us; the launch traced here: 756 us
  waiting for transfers between devices  629 us (83%)
  matrix products  61.9 us (8%)
  local copies, waits for them, and re-layouts  33.3 us (4%)
  between operations  15.4 us (2%)
  other arithmetic  12.2 us (2%)
    unnamed x10, waiting for transfers between devices  342 us
    all_gather x6, waiting for transfers between devices, slot_pass(): lax.all_gather(shards[head_index].astype(jnp.bfloat16), 'shard', axis=0,...  282 us
    another operation x6, local copies, waits for them, and re-layouts, head_pass(): jnp.stack([gate_part, up_part, down_part], axis=1)  21.3 us
    dot_general x12, matrix products, forward(): lax.dot_general(hidden, packed[:, 2], (((1,), (1,)), ((), ())), preferred...  19.7 us
    dot_general x12, matrix products, forward(): pre_gate = jnp.dot(rows, packed[:, 0], preferred_element_type=jnp.float32)  15.2 us
  transfers between devices with their start and end apart: 9, of which 9 were waited for; matrix products, arithmetic and copies ran while one was open for 7% of the time, Pallas kernels for 0%

commit v1 on v0

--- a/solution.py
+++ b/solution.py
@@ -2,6 +2,7 @@
 import jax.numpy as jnp
 from jax import lax
 from jax.sharding import PartitionSpec as P
+from jax.lax import all_to_all, axis_size
 
 epsilon = 1e-06
 
@@ -66,9 +67,12 @@
         updates = []
         arrivals = []
         for head_index in range(head_count):
-            packed = lax.all_gather(
-                shards[head_index].astype(jnp.bfloat16), "shard", axis=0, tiled=True
-            )
+
+            def _keep_up_rings(my_tile):
+                arr_out = jnp.stack([my_tile for _ in range(axis_size("shard"))], axis=0)
+                return jnp.concatenate(all_to_all(arr_out, "shard", 0, 0), axis=0)
+
+            packed = _keep_up_rings(shards[head_index].astype(jnp.bfloat16))
             normed, updated = head_pass(slot_index, head_index, packed, shards[head_index])
             outputs.append(normed)
             updates.append(updated)

time: 757 us -> 627 us (0.83)
  waiting for transfers between devices: 629 us -> 463 us
  starting transfers between devices: 4.09 us -> 32.4 us
  local copies, waits for them, and re-layouts: 33.3 us -> 46.9 us
    all_gather x6 -> x0, waiting for transfers between devices: 282 us -> none  [slot_pass(): lax.all_gather(shards[head_index].astype(jnp.bfloat16), 'shard', axis=0,...]
    all_to_all x0 -> x6, waiting for transfers between devices: none -> 117 us  [_keep_up_rings(): return jnp.concatenate(all_to_all(arr_out, 'shard', 0, 0), axis=0)]
    all_to_all x0 -> x6, starting transfers between devices: none -> 28.6 us  [_keep_up_rings(): return jnp.concatenate(all_to_all(arr_out, 'shard', 0, 0), axis=0)]
    all_to_all x0 -> x6, local copies, waits for them, and re-layouts: none -> 9.21 us  [_keep_up_rings(): return jnp.concatenate(all_to_all(arr_out, 'shard', 0, 0), axis=0)]
    another operation x0 -> x16, local copies, waits for them, and re-layouts: none -> 8.89 us  [the longest x10 8.61 us: _keep_up_rings(): arr_out = jnp.stack([my_tile for _ in range(axis_size('shard'))], axis=0)]
    unnamed x10 -> x4, waiting for transfers between devices: 342 us -> 340 us
where the time goes in v1:
time: 627 us; the launch traced here: 626 us
  waiting for transfers between devices  463 us (74%)
  matrix products  58.7 us (9%)
  local copies, waits for them, and re-layouts  46.9 us (7%)
  starting transfers between devices  32.4 us (5%)
  between operations  15.7 us (3%)
  other arithmetic  9.46 us (2%)
    unnamed x4, waiting for transfers between devices  340 us
    all_to_all x6, waiting for transfers between devices, _keep_up_rings(): return jnp.concatenate(all_to_all(arr_out, 'shard', 0, 0), axis=0)  117 us
    all_to_all x6, starting transfers between devices, _keep_up_rings(): return jnp.concatenate(all_to_all(arr_out, 'shard', 0, 0), axis=0)  28.6 us
    another operation x6, local copies, waits for them, and re-layouts, head_pass(): jnp.stack([gate_part, up_part, down_part], axis=1)  21.4 us
    dot_general x12, matrix products, forward(): lax.dot_general(hidden, packed[:, 2], (((1,), (1,)), ((), ())), preferred...  19.6 us
  transfers between devices with their start and end apart: 9, of which 9 were waited for; matrix products, arithmetic and copies ran while one was open for 7% of the time, Pallas kernels for 0%

profile of v1, /device:TPU:32, one launch (start us, length us, event | category | flops | bytes accessed | tf_op | source)
XLA Modules:
  0.0 625.8 jit_solution(18220433987506013607)
XLA Ops:
  10.7 7.0 %all-to-all-start.1 = ((bf16[16,32,3,512]{3,1,2,0:T(8,128)(2,1)}), bf16[16,32,3,512]{3,1,2,0:T(8,128)(2,1)S(1)}, u32[]{:S(2)}, u32[]{:S(2)}) async-start(bf16[16,32,3,512]{3,1,2,0:T(8,128)(2,1)} %stack.110), calls=%async_computation.1 | async-start | bytes 3145728 | tf_op jit(solution)/shard_map/all_to_all | solution.py:73
  17.8 23.6 %all-to-all-done.1 = bf16[16,32,3,512]{3,1,2,0:T(8,128)(2,1)S(1)} async-done(((bf16[16,32,3,512]{3,1,2,0:T(8,128)(2,1)}), bf16[16,32,3,512]{3,1,2,0:T(8,128)(2,1)S(1)}, u32[]{:S(2)}, u32[]{:S(2)}) %all-to-all-start.1) | async-done | bytes 1572896 | tf_op jit(solution)/shard_map/all_to_all | solution.py:73
  43.0 4.4 all-to-all-start.2
  47.7 1.6 copy.66
  51.8 19.4 %all-to-all-done.2 = bf16[16,32,3,512]{3,1,2,0:T(8,128)(2,1)} async-done(((bf16[16,32,3,512]{3,1,2,0:T(8,128)(2,1)}), bf16[16,32,3,512]{3,1,2,0:T(8,128)(2,1)}, u32[]{:S(2)}, u32[]{:S(2)}) %all-to-all-start.2) | async-done | bytes 1572896 | tf_op jit(solution)/shard_map/all_to_all | solution.py:73
  72.5 4.4 all-to-all-start
  78.5 1.5 convolution_bitcast_fusion.12
  85.0 15.6 %all-to-all-done = bf16[16,32,3,512]{3,1,2,0:T(8,128)(2,1)} async-done(((bf16[16,32,3,512]{3,1,2,0:T(8,128)(2,1)}), bf16[16,32,3,512]{3,1,2,0:T(8,128)(2,1)}, u32[]{:S(2)}, u32[]{:S(2)}) %all-to-all-start) | async-done | bytes 1572896 | tf_op jit(solution)/shard_map/all_to_all | solution.py:73
  108.4 3.5 copy.73
  115.0 3.6 copy.75
  121.7 3.6 copy.71
  127.2 180.4 %all-reduce.13.cloned.1.call-done = (f32[512,3,512]{2,1,0:T(4,128)}, f32[512,3,512]{2,1,0:T(4,128)}, f32[512,3,512]{2,1,0:T(4,128)}) async-done(((f32[512,3,512]{2,1,0:T(4,128)}, f32[512,3,512]{2,1,0:T(4,128)}, f32[512,3,512]{2,1,0:T(4,128)}), (f32[512,3,512]{2,1,0:T(4,128)}, f32[512,3,512]{2,1,0:T(4,128)}, f32[512,3,512]{2,1,0:T(4,128)})) %all-reduce.13.cloned.1.call-update) | async-done | bytes 9437200
  311.1 3.5 collective-permute-start
  314.6 5.1 collective-permute-done
  322.7 4.0 all-to-all-start.4
  326.7 23.6 %all-to-all-done.4 = bf16[16,32,3,512]{3,1,2,0:T(8,128)(2,1)S(1)} async-done(((bf16[16,32,3,512]{3,1,2,0:T(8,128)(2,1)}), bf16[16,32,3,512]{3,1,2,0:T(8,128)(2,1)S(1)}, u32[]{:S(2)}, u32[]{:S(2)}) %all-to-all-start.4) | async-done | bytes 1572896 | tf_op jit(solution)/shard_map/all_to_all | solution.py:73
  352.0 4.4 all-to-all-start.5
  356.4 1.6 copy.86
  360.5 19.6 %all-to-all-done.5 = bf16[16,32,3,512]{3,1,2,0:T(8,128)(2,1)} async-done(((bf16[16,32,3,512]{3,1,2,0:T(8,128)(2,1)}), bf16[16,32,3,512]{3,1,2,0:T(8,128)(2,1)}, u32[]{:S(2)}, u32[]{:S(2)}) %all-to-all-start.5) | async-done | bytes 1572896 | tf_op jit(solution)/shard_map/all_to_all | solution.py:73
  381.4 4.4 all-to-all-start.3
  387.6 1.6 convolution_bitcast_fusion.3
  394.1 15.4 %all-to-all-done.3 = bf16[16,32,3,512]{3,1,2,0:T(8,128)(2,1)} async-done(((bf16[16,32,3,512]{3,1,2,0:T(8,128)(2,1)}), bf16[16,32,3,512]{3,1,2,0:T(8,128)(2,1)}, u32[]{:S(2)}, u32[]{:S(2)}) %all-to-all-start.3) | async-done | bytes 1572896 | tf_op jit(solution)/shard_map/all_to_all | solution.py:73
  417.4 3.5 copy.100
  424.0 3.6 copy.104
  430.7 3.6 copy.96
  436.8 2.2 multiply_reduce_fusion.4
  440.1 2.2 multiply_reduce_fusion.3
  443.5 2.2 multiply_reduce_fusion.5
  446.8 2.2 multiply_reduce_fusion.1
  450.1 2.2 multiply_reduce_fusion
  453.5 1.5 multiply_reduce_fusion.2
  456.6 159.9 %all-reduce.11.cloned.1.call-done = (f32[512,3,512]{2,1,0:T(4,128)}, f32[512,3,512]{2,1,0:T(4,128)}, f32[512,3,512]{2,1,0:T(4,128)}) async-done(((f32[512,3,512]{2,1,0:T(4,128)}, f32[512,3,512]{2,1,0:T(4,128)}, f32[512,3,512]{2,1,0:T(4,128)}), (f32[512,3,512]{2,1,0:T(4,128)}, f32[512,3,512]{2,1,0:T(4,128)}, f32[512,3,512]{2,1,0:T(4,128)})) %all-reduce.11.cloned.1.call-update) | async-done | bytes 9437200
  (210 shorter events, 75.3 us)
Async XLA Ops:
  8.4 39.1 %copy-start.32 = (f32[1,1,32,3,512]{4,2,3,1,0:T(8,128)}, f32[1,1,32,3,512]{4,2,3,1,0:T(8,128)S(1)}, u32[]{:S(2)}) copy-start(f32[1,1,32,3,512]{4,2,3,1,0:T(8,128)S(1)} %get-tuple-element.18) | copy-start | bytes 589828
  10.7 30.7 %all-to-all-start.1 = ((bf16[16,32,3,512]{3,1,2,0:T(8,128)(2,1)}), bf16[16,32,3,512]{3,1,2,0:T(8,128)(2,1)S(1)}, u32[]{:S(2)}, u32[]{:S(2)}) async-start(bf16[16,32,3,512]{3,1,2,0:T(8,128)(2,1)} %stack.110), calls=%async_computation.1 | async-start | bytes 3145728 | tf_op jit(solution)/shard_map/all_to_all | solution.py:73
  42.9 4.8 copy-start.51
  43.0 28.1 %all-to-all-start.2 = ((bf16[16,32,3,512]{3,1,2,0:T(8,128)(2,1)}), bf16[16,32,3,512]{3,1,2,0:T(8,128)(2,1)}, u32[]{:S(2)}, u32[]{:S(2)}) async-start(bf16[16,32,3,512]{3,1,2,0:T(8,128)(2,1)} %stack.112), calls=%async_computation.2 | async-start | bytes 3145728 | tf_op jit(solution)/shard_map/all_to_all | solution.py:73
  49.3 34.5 %copy-start.2 = (bf16[16,32,3,512]{3,1,0,2:T(8,128)(2,1)}, bf16[16,32,3,512]{3,1,0,2:T(8,128)(2,1)S(1)}, u32[]{:S(2)}) copy-start(bf16[16,32,3,512]{3,1,0,2:T(8,128)(2,1)S(1)} %copy.66) | copy-start | bytes 4718596
  72.5 28.1 %all-to-all-start = ((bf16[16,32,3,512]{3,1,2,0:T(8,128)(2,1)}), bf16[16,32,3,512]{3,1,2,0:T(8,128)(2,1)}, u32[]{:S(2)}, u32[]{:S(2)}) async-start(bf16[16,32,3,512]{3,1,2,0:T(8,128)(2,1)} %stack.108), calls=%async_computation | async-start | bytes 3145728 | tf_op jit(solution)/shard_map/all_to_all | solution.py:73
  76.9 230.6 %all-reduce.13.cloned.1.call-start = ((), (), s32[]{:S(2)}) async-start(), calls=%async_computation.7 | async-start | bytes 25165824
  78.5 5.5 copy-start.4
  102.1 2.6 copy-start.6
  102.3 3.3 copy-start.26
  112.0 2.7 copy-start.19
  115.0 3.6 copy-start.27
  118.6 2.7 copy-start.22
  125.3 182.3 %copy-start.33 = (f32[1,1,32,3,512]{4,2,3,1,0:T(8,128)S(1)}, f32[1,1,32,3,512]{4,2,3,1,0:T(8,128)}, u32[]{:S(2)}) copy-start(f32[1,1,32,3,512]{4,2,3,1,0:T(8,128)} %copy-done.32) | copy-start | bytes 589828
  125.3 183.4 %copy-start.37 = (f32[1,1,32,3,512]{4,2,3,1,0:T(8,128)S(1)}, f32[1,1,32,3,512]{4,2,3,1,0:T(8,128)}, u32[]{:S(2)}) copy-start(f32[1,1,32,3,512]{4,2,3,1,0:T(8,128)} %copy-done.36) | copy-start | bytes 589828
  125.3 184.5 %copy-start.35 = (f32[1,1,32,3,512]{4,2,3,1,0:T(8,128)S(1)}, f32[1,1,32,3,512]{4,2,3,1,0:T(8,128)}, u32[]{:S(2)}) copy-start(f32[1,1,32,3,512]{4,2,3,1,0:T(8,128)} %copy-done.34) | copy-start | bytes 589828
  125.3 194.4 %copy-start.38 = (f32[3,32,3,512]{3,1,2,0:T(8,128)S(1)}, f32[3,32,3,512]{3,1,2,0:T(8,128)}, u32[]{:S(2)}) copy-start(f32[3,32,3,512]{3,1,2,0:T(8,128)} %param.12) | copy-start | bytes 1769476
  311.1 8.6 %collective-permute-start = (bf16[3,32,3,512]{3,1,2,0:T(8,128)(2,1)S(1)}, bf16[3,32,3,512]{3,1,2,0:T(8,128)(2,1)S(1)}, u32[]{:S(2)}, u32[]{:S(2)}) collective-permute-start(bf16[3,32,3,512]{3,1,2,0:T(8,128)(2,1)S(1)} %pad_maximum_fusion.7), channel_id=1, source_target_pairs={{0,16},{16,32},{32,48},{48,64},{64,80},{80,96},{96,112},{112,128},... | collective-permute-start | bytes 884744 | tf_op jit(solution)/shard_map/ppermute | solution.py:13
  322.7 27.6 %all-to-all-start.4 = ((bf16[16,32,3,512]{3,1,2,0:T(8,128)(2,1)}), bf16[16,32,3,512]{3,1,2,0:T(8,128)(2,1)S(1)}, u32[]{:S(2)}, u32[]{:S(2)}) async-start(bf16[16,32,3,512]{3,1,2,0:T(8,128)(2,1)} %stack.136), calls=%async_computation.4 | async-start | bytes 3145728 | tf_op jit(solution)/shard_map/all_to_all | solution.py:73
  352.0 28.1 %all-to-all-start.5 = ((bf16[16,32,3,512]{3,1,2,0:T(8,128)(2,1)}), bf16[16,32,3,512]{3,1,2,0:T(8,128)(2,1)}, u32[]{:S(2)}, u32[]{:S(2)}) async-start(bf16[16,32,3,512]{3,1,2,0:T(8,128)(2,1)} %stack.139), calls=%async_computation.5 | async-start | bytes 3145728 | tf_op jit(solution)/shard_map/all_to_all | solution.py:73
  358.0 34.9 %copy-start.8 = (bf16[16,32,3,512]{3,1,0,2:T(8,128)(2,1)}, bf16[16,32,3,512]{3,1,0,2:T(8,128)(2,1)S(1)}, u32[]{:S(2)}) copy-start(bf16[16,32,3,512]{3,1,0,2:T(8,128)(2,1)S(1)} %copy.86) | copy-start | bytes 4718596
  381.4 28.1 %all-to-all-start.3 = ((bf16[16,32,3,512]{3,1,2,0:T(8,128)(2,1)}), bf16[16,32,3,512]{3,1,2,0:T(8,128)(2,1)}, u32[]{:S(2)}, u32[]{:S(2)}) async-start(bf16[16,32,3,512]{3,1,2,0:T(8,128)(2,1)} %stack.133), calls=%async_computation.3 | async-start | bytes 3145728 | tf_op jit(solution)/shard_map/all_to_all | solution.py:73
  385.8 230.7 %all-reduce.11.cloned.1.call-start = ((), (), s32[]{:S(2)}) async-start(), calls=%async_computation.6 | async-start | bytes 25165824
  387.6 5.6 copy-start.10
  411.0 2.6 copy-start.12
  411.3 3.3 copy-start.24
  420.9 2.7 copy-start.18
  424.0 3.6 copy-start.25
  427.6 2.7 copy-start.23
  443.5 2.2 copy-start.9
  450.1 2.2 copy-start.13
  455.5 161.0 %copy-start.17 = (f32[3,32,3,512]{3,2,1,0:T(4,128)S(1)}, f32[3,32,3,512]{3,2,1,0:T(4,128)}, u32[]{:S(2)}) copy-start(f32[3,32,3,512]{3,2,1,0:T(4,128)} %copy-done.16) | copy-start | bytes 1769476
  (30 other events, 44.2 us)
Sparse Core Ops, SparseCore 0:
  125.4 182.0 all-reduce.12
  434.4 182.0 all-reduce.10
